TPU v7x, 32 devices: a whole 2x2x4 slice. The times are simulated.
32 devices in a mesh: grp: 2 (over x), ctr: 16 (over z, y, core).
Axes of the slice: x: 2, y: 2, z: 4, core: 2. Of those that a mesh axis runs over, the one named last changes fastest.
Arguments:
- centres: bfloat16 [6144, 768], P(('grp', 'ctr')), parts along dimension 0
- sample_idx: int32 [1024], P(('grp', 'ctr')), parts along dimension 0, may hold values from 0 to 3071, as said below
- coef: float32 [6144], P(('grp', 'ctr')), parts along dimension 0
- metric_factor: bfloat16 [768, 768], replicated, may hold values from -0.21875 to 0.21875
Outputs:
- metric_new: float32 [1536, 768], P(('grp', 'ctr')), parts along dimension 0
- transformed: float32 [1024, 768], P(('grp', 'ctr')), parts along dimension 0
There are 2 independent parts, one for each index of `grp`. A program takes and returns all parts, laid end to end along the dimension named above; an argument that names none is the same for every part. Nothing has to cross between parts.
Inputs may be any that keep to these rules, and one draw needn't show every extreme that they name: The 32 samples of the k-th aligned block of sample_idx are distinct centres of the k-th block of 192 centres.
All inputs are finite; a program needn't handle non-finite values.
Results may differ from a plain program's by a relative error of at most 0.0031.
Values may be sent and summed in bfloat16 or wider, within the bound.
A program may use at most 128 MiB of HBM per device.

v0:
```python
import jax
import jax.numpy as jnp
from jax import lax
from jax.sharding import PartitionSpec as P


def block_grad(rows_u, v_own, sv_own, coef):
    width = rows_u.shape[1]
    su = jnp.sum(rows_u.astype(jnp.float32) ** 2, axis=1)
    cross = jnp.dot(rows_u, v_own.T, preferred_element_type=jnp.float32)
    dist_sq = jnp.maximum(su[:, None] + sv_own[None, :] - 2.0 * cross, 0.0)
    radius = jnp.sqrt(dist_sq / width + 1.0)
    weight = coef[None, :] * jnp.exp(-radius / 4.0) / (4.0 * width * radius)
    wround = weight.astype(jnp.bfloat16)
    return jnp.dot(wround, v_own, preferred_element_type=jnp.float32) - jnp.sum(weight, axis=1)[
        :, None
    ] * rows_u.astype(jnp.float32)


def local(centres, sample_idx, coef, metric_factor):
    width = centres.shape[1]
    own_count = sample_idx.shape[0]
    devices = lax.axis_size("ctr")
    offset = lax.axis_index("ctr") * centres.shape[0]
    own_rows = jnp.take(centres, sample_idx - offset, axis=0)
    u_own = jnp.dot(own_rows, metric_factor, preferred_element_type=jnp.float32).astype(
        jnp.bfloat16
    )
    v_own = jnp.dot(centres, metric_factor, preferred_element_type=jnp.float32).astype(jnp.bfloat16)
    factor = metric_factor.astype(jnp.float32)
    coef_full = lax.all_gather(coef, "ctr", axis=0, tiled=True)
    piece = lax.all_gather(v_own, "ctr", axis=0, tiled=True)
    sv_piece = jnp.sum(piece.astype(jnp.float32) ** 2, axis=1)
    summed = block_grad(u_own, piece, sv_piece, coef_full)
    grads = jnp.dot(summed, factor.T, precision=lax.Precision.HIGHEST)
    local_outer = jnp.dot(grads.T, grads, precision=lax.Precision.HIGHEST) / (own_count * devices)
    agop = lax.psum(local_outer, "ctr")
    metric_full = agop * width / jnp.trace(agop)
    row_count = width // devices
    metric_rows = lax.dynamic_slice_in_dim(
        metric_full, lax.axis_index("ctr") * row_count, row_count, 0
    )
    transformed = jnp.dot(grads, metric_full, precision=lax.Precision.HIGHEST)
    return (metric_rows, transformed)


def solution(mesh):
    placed = (P(("grp", "ctr"), None), P(("grp", "ctr")), P(("grp", "ctr")), P())
    return jax.shard_map(
        local,
        mesh=mesh,
        in_specs=placed,
        out_specs=(P(("grp", "ctr"), None), P(("grp", "ctr"), None)),
        check_vma=False,
    )
```

profile of v0, /device:TPU:0, one launch (start us, length us, event | category | flops | bytes accessed | tf_op | source)
XLA Modules:
  0.0 199.3 jit_solution(7842170020570275571)
XLA Ops:
  7.2 0.0 copy-start
  7.2 0.0 copy-start.4
  7.2 0.0 copy-start.3
  7.2 0.0 all-gather.2.cloned.1.call-start
  7.2 1.2 copy-done
  8.4 2.1 %convolution_convert_fusion = bf16[192,768]{1,0:T(8,128)(2,1)} fusion(bf16[192,768]{1,0:T(8,128)(2,1)} %param.4, bf16[768,768]{1,0:T(8,128)(2,1)S(1)} %copy-done), kind=kOutput, calls=%fused_computation.12 | convolution fusion | flops 226639872 | bytes 1769472 | tf_op jit(solution)/shard_map/dot_general | solution.py:29
  10.5 0.0 all-gather.2.cloned.1.call-update
  10.5 0.0 all-reduce.3.cloned.1.call-start
  10.6 0.7 compare_and_fusion
  11.3 1.7 gather_fusion
  12.9 0.0 copy-done.4
  12.9 0.6 dynamic-slice
  14.2 0.0 copy-done.3
  14.2 0.3 dynamic-update-slice
  14.5 64.2 %all-reduce = f32[3072]{0:T(1024)S(1)} all-reduce(f32[3072]{0:T(1024)S(1)} %dynamic-update-slice), channel_id=1, replica_groups=mesh['grp'=2,'ctr'=16] {'ctr'}, use_global_device_ids=true, to_apply=%add | all-reduce | flops 3072 | bytes 24576
  78.7 0.5 fusion.6
  79.1 0.0 all-gather.2.cloned.1.call-done
  79.2 0.0 copy-start.1
  79.2 3.5 %multiply_reduce_fusion = f32[3072]{0:T(1024)S(1)} fusion(bf16[3072,768]{1,0:T(8,128)(2,1)} %all-gather.2.cloned.1.call-done), kind=kLoop, calls=%fused_computation.1 | loop fusion | flops 7074816 | bytes 4730880 | tf_op jit(solution)/shard_map/reduce_sum | solution.py:33
  82.7 0.3 copy-done.1
  82.9 1.7 fusion.11
  84.6 0.9 convolution_subtract_fusion
  85.4 1.1 fusion.12
  86.6 3.5 %convolution_multiply_fusion.1 = f32[768,768]{1,0:T(8,128)} fusion(f32[32,768]{1,0:T(8,128)S(1)} %fusion.12), kind=kOutput, calls=%fused_computation.11 | convolution fusion | flops 227082240 | bytes 2457600 | tf_op jit(solution)/shard_map/dot_general | solution.py:36
  90.1 0.0 all-reduce.3.cloned.1.call-update
  90.1 96.2 %all-reduce.3.cloned.1.call-done = f32[768,768]{1,0:T(8,128)} async-done(((f32[768,768]{1,0:T(8,128)}), f32[768,768]{1,0:T(8,128)}) %all-reduce.3.cloned.1.call-update) | async-done | bytes 2359312 | tf_op jit(solution)/shard_map/psum | solution.py:37
  186.3 0.0 copy-start.2
  186.3 2.5 %select_reduce_fusion = f32[]{:T(128)} fusion(f32[768,768]{1,0:T(8,128)} %all-reduce.3.cloned.1.call-done), kind=kLoop, calls=%fused_computation.8 | loop fusion | flops 1769471 | bytes 2359300 | tf_op jit(solution)/shard_map/jit(trace)/reduce_sum | solution.py:38
  188.8 0.0 copy-done.2
  188.8 0.8 multiply_divide_fusion
  189.7 2.1 %fusion.13 = f32[32,768]{1,0:T(8,128)} fusion(f32[32,768]{1,0:T(8,128)S(1)} %fusion.12, f32[768,768]{1,0:T(8,128)S(1)} %multiply_divide_fusion), kind=kOutput, calls=%fused_computation.30 | convolution fusion | flops 226492416 | bytes 2555904 | tf_op jit(solution)/shard_map/dot_general | solution.py:43
  191.7 0.7 constant_dynamic-slice_fusion
  (2 shorter events, 0.0 us)
Async XLA Ops:
  7.2 1.3 copy-start
  7.2 5.8 %copy-start.4 = (u32[32]{0:T(128)S(1)}, u32[32]{0:T(128)}, u32[]{:S(2)}) copy-start(u32[32]{0:T(128)} %constant.52) | copy-start | bytes 388
  7.2 7.0 %copy-start.3 = (f32[192]{0:T(256)S(1)}, f32[192]{0:T(256)}, u32[]{:S(2)}) copy-start(f32[192]{0:T(256)} %param.6) | copy-start | bytes 2308
  7.2 72.0 %all-gather.2.cloned.1.call-start = ((), (), s32[]{:S(2)}) async-start(), calls=%async_computation | async-start | bytes 5013504 | tf_op jit(solution)/shard_map/all_gather | solution.py:32
  10.5 175.8 %all-reduce.3.cloned.1.call-start = ((), (), s32[]{:S(2)}) async-start(), calls=%async_computation.1 | async-start | bytes 4718592 | tf_op jit(solution)/shard_map/psum | solution.py:37
  79.2 3.8 %copy-start.1 = (bf16[3072,768]{1,0:T(8,128)(2,1)S(1)}, bf16[3072,768]{1,0:T(8,128)(2,1)}, u32[]{:S(2)}) copy-start(bf16[3072,768]{1,0:T(8,128)(2,1)} %all-gather.2.cloned.1.call-done) | copy-start | bytes 14155780
  186.3 2.5 %copy-start.2 = (f32[768,768]{1,0:T(8,128)S(1)}, f32[768,768]{1,0:T(8,128)}, u32[]{:S(2)}) copy-start(f32[768,768]{1,0:T(8,128)} %all-reduce.3.cloned.1.call-done) | copy-start | bytes 7077892
Sparse Core Ops, SparseCore 0:
  10.7 56.3 all-gather.1
  90.2 96.0 all-reduce.2
where the time goes:
time: 200 us; the launch traced here: 199 us
  waiting for transfers between devices  96.3 us (48%)
  blocking collectives  64.2 us (32%)
  between operations  14.8 us (7%)
  matrix products  11.8 us (6%)
  other arithmetic  7.48 us (4%)
  local copies, waits for them, and re-layouts  4.68 us (2%)
    psum x1, waiting for transfers between devices, local(): agop = lax.psum(local_outer, 'ctr')  96.2 us
    unnamed x1, blocking collectives  64.2 us
  transfers between devices with their start and end apart: 2, of which 1 were waited for; matrix products, arithmetic and copies ran while one was open for 2% of the time, Pallas kernels for 0%

commit v1 on v0

--- a/solution.py
+++ b/solution.py
@@ -2,6 +2,14 @@
 import jax.numpy as jnp
 from jax import lax
 from jax.sharding import PartitionSpec as P
+
+
+def added_up(x, axis):
+    n_dev, result = (lax.axis_size(axis), x)
+    for hop in [1 << k for k in range(n_dev.bit_length() - 1)]:
+        pairs = [(i, i ^ hop) for i in range(n_dev)]
+        result = result + lax.ppermute(result, axis, pairs)
+    return result
 
 
 def block_grad(rows_u, v_own, sv_own, coef):
@@ -34,7 +42,7 @@
     summed = block_grad(u_own, piece, sv_piece, coef_full)
     grads = jnp.dot(summed, factor.T, precision=lax.Precision.HIGHEST)
     local_outer = jnp.dot(grads.T, grads, precision=lax.Precision.HIGHEST) / (own_count * devices)
-    agop = lax.psum(local_outer, "ctr")
+    agop = added_up(local_outer, "ctr")
     metric_full = agop * width / jnp.trace(agop)
     row_count = width // devices
     metric_rows = lax.dynamic_slice_in_dim(

time: 200 us -> 318 us (1.59)
  waiting for transfers between devices: 96.3 us -> 213 us
    ppermute x0 -> x4, waiting for transfers between devices: none -> 213 us  [added_up(): result = result + lax.ppermute(result, axis, pairs)]
    psum x1 -> x0, waiting for transfers between devices: 96.2 us -> none  [local(): agop = lax.psum(local_outer, 'ctr')]
  transfers between devices with their start and end apart: 2 -> 5, of which waited for: 1 -> 4; matrix products, arithmetic and copies ran while one was open for 2% -> 1% of each run, Pallas kernels for 0% -> 0%
where the time goes in v1:
time: 318 us
  waiting for transfers between devices  213 us (67%)
  blocking collectives  64.2 us (20%)
  between operations  14.9 us (5%)
  matrix products  10.4 us (3%)
  other arithmetic  10 us (3%)
  local copies, waits for them, and re-layouts  4.68 us (1%)
    ppermute x4, waiting for transfers between devices, added_up(): result = result + lax.ppermute(result, axis, pairs)  213 us
    unnamed x1, blocking collectives  64.2 us
  transfers between devices with their start and end apart: 5, of which 4 were waited for; matrix products, arithmetic and copies ran while one was open for 1% of the time, Pallas kernels for 0%

profile of v1, /device:TPU:0, one launch (start us, length us, event | category | flops | bytes accessed | tf_op | source)
XLA Modules:
  0.0 317.8 jit_solution(11110390465922464809)
XLA Ops:
  7.2 0.0 copy-start
  7.2 0.0 copy-start.5
  7.2 0.0 copy-start.4
  7.2 0.0 all-gather.2.cloned.1.call-start
  7.2 1.2 copy-done
  8.4 2.1 convolution_convert_fusion
  10.5 0.0 all-gather.2.cloned.1.call-update
  10.6 0.7 compare_and_fusion
  11.2 1.7 gather_fusion
  12.9 0.0 copy-done.5
  12.9 0.6 dynamic-slice
  14.2 0.0 copy-done.4
  14.2 0.3 dynamic-update-slice
  14.4 64.2 %all-reduce = f32[3072]{0:T(1024)S(1)} all-reduce(f32[3072]{0:T(1024)S(1)} %dynamic-update-slice), channel_id=1, replica_groups=mesh['grp'=2,'ctr'=16] {'ctr'}, use_global_device_ids=true, to_apply=%add | all-reduce | flops 3072 | bytes 24576
  78.6 0.5 fusion.6
  79.1 0.0 all-gather.2.cloned.1.call-done
  79.1 0.0 copy-start.1
  79.1 3.5 %multiply_reduce_fusion = f32[3072]{0:T(1024)S(1)} fusion(bf16[3072,768]{1,0:T(8,128)(2,1)} %all-gather.2.cloned.1.call-done), kind=kLoop, calls=%fused_computation.1 | loop fusion | flops 7074816 | bytes 4730880 | tf_op jit(solution)/shard_map/reduce_sum | solution.py:41
  82.6 0.3 copy-done.1
  82.9 1.6 fusion.11
  84.5 0.9 convolution_subtract_fusion
  85.4 1.1 fusion.12
  86.5 0.0 copy-start.2
  86.5 2.1 convolution_multiply_fusion.1
  88.7 0.1 collective-permute-start
  88.7 0.0 copy-done.2
  88.8 4.5 %collective-permute-done = f32[768,768]{1,0:T(8,128)S(1)} collective-permute-done((f32[768,768]{1,0:T(8,128)S(1)}, f32[768,768]{1,0:T(8,128)S(1)}, u32[]{:S(2)}, u32[]{:S(2)}) %collective-permute-start) | collective-permute-done | bytes 2359328 | tf_op jit(solution)/shard_map/ppermute | solution.py:11
  93.3 0.3 add.49
  93.6 0.1 collective-permute-start.1
  93.6 53.3 %collective-permute-done.1 = f32[768,768]{1,0:T(8,128)S(1)} collective-permute-done((f32[768,768]{1,0:T(8,128)S(1)}, f32[768,768]{1,0:T(8,128)S(1)}, u32[]{:S(2)}, u32[]{:S(2)}) %collective-permute-start.1) | collective-permute-done | bytes 2359328 | tf_op jit(solution)/shard_map/ppermute | solution.py:11
  146.9 0.3 add.50
  147.2 0.1 collective-permute-start.2
  147.3 52.4 %collective-permute-done.2 = f32[768,768]{1,0:T(8,128)S(1)} collective-permute-done((f32[768,768]{1,0:T(8,128)S(1)}, f32[768,768]{1,0:T(8,128)S(1)}, u32[]{:S(2)}, u32[]{:S(2)}) %collective-permute-start.2) | collective-permute-done | bytes 2359328 | tf_op jit(solution)/shard_map/ppermute | solution.py:11
  199.7 0.3 add.51
  200.0 0.1 collective-permute-start.3
  200.1 103.1 %collective-permute-done.3 = f32[768,768]{1,0:T(8,128)} collective-permute-done((f32[768,768]{1,0:T(8,128)S(1)}, f32[768,768]{1,0:T(8,128)}, u32[]{:S(2)}, u32[]{:S(2)}) %collective-permute-start.3) | collective-permute-done | bytes 2359328 | tf_op jit(solution)/shard_map/ppermute | solution.py:11
  303.2 2.4 select_reduce_fusion
  305.6 0.0 copy-start.3
  305.6 2.6 multiply_divide_fusion
  308.2 0.0 copy-done.3
  308.2 2.1 fusion.13
  310.3 0.7 constant_dynamic-slice_fusion
  (2 shorter events, 0.0 us)
Async XLA Ops:
  7.2 1.3 copy-start
  7.2 5.7 %copy-start.5 = (u32[32]{0:T(128)S(1)}, u32[32]{0:T(128)}, u32[]{:S(2)}) copy-start(u32[32]{0:T(128)} %constant.52) | copy-start | bytes 388
  7.2 7.0 %copy-start.4 = (f32[192]{0:T(256)S(1)}, f32[192]{0:T(256)}, u32[]{:S(2)}) copy-start(f32[192]{0:T(256)} %param.6) | copy-start | bytes 2308
  7.2 71.9 %all-gather.2.cloned.1.call-start = ((), (), s32[]{:S(2)}) async-start(), calls=%async_computation | async-start | bytes 5013504 | tf_op jit(solution)/shard_map/all_gather | solution.py:40
  79.1 3.8 %copy-start.1 = (bf16[3072,768]{1,0:T(8,128)(2,1)S(1)}, bf16[3072,768]{1,0:T(8,128)(2,1)}, u32[]{:S(2)}) copy-start(bf16[3072,768]{1,0:T(8,128)(2,1)} %all-gather.2.cloned.1.call-done) | copy-start | bytes 14155780
  86.5 2.2 copy-start.2
  88.7 4.6 %collective-permute-start = (f32[768,768]{1,0:T(8,128)S(1)}, f32[768,768]{1,0:T(8,128)S(1)}, u32[]{:S(2)}, u32[]{:S(2)}) collective-permute-start(f32[768,768]{1,0:T(8,128)S(1)} %convolution_multiply_fusion.1), channel_id=1, source_target_pairs={{0,1},{1,0},{2,3},{3,2},{4,5},{5,4},{6,7},{7,6},{8,9},{9,8},{10,11... | collective-permute-start | bytes 7077896 | tf_op jit(solution)/shard_map/ppermute | solution.py:11
  93.6 53.4 %collective-permute-start.1 = (f32[768,768]{1,0:T(8,128)S(1)}, f32[768,768]{1,0:T(8,128)S(1)}, u32[]{:S(2)}, u32[]{:S(2)}) collective-permute-start(f32[768,768]{1,0:T(8,128)S(1)} %add.49), channel_id=1, source_target_pairs={{0,2},{1,3},{2,0},{3,1},{4,6},{5,7},{6,4},{7,5},{8,10},{9,11},{10,... | collective-permute-start | bytes 7077896 | tf_op jit(solution)/shard_map/ppermute | solution.py:11
  147.2 52.5 %collective-permute-start.2 = (f32[768,768]{1,0:T(8,128)S(1)}, f32[768,768]{1,0:T(8,128)S(1)}, u32[]{:S(2)}, u32[]{:S(2)}) collective-permute-start(f32[768,768]{1,0:T(8,128)S(1)} %add.50), channel_id=1, source_target_pairs={{0,4},{1,5},{2,6},{3,7},{4,0},{5,1},{6,2},{7,3},{8,12},{9,13},{10,... | collective-permute-start | bytes 7077896 | tf_op jit(solution)/shard_map/ppermute | solution.py:11
  200.0 103.2 %collective-permute-start.3 = (f32[768,768]{1,0:T(8,128)S(1)}, f32[768,768]{1,0:T(8,128)}, u32[]{:S(2)}, u32[]{:S(2)}) collective-permute-start(f32[768,768]{1,0:T(8,128)S(1)} %add.51), channel_id=1, source_target_pairs={{0,8},{1,9},{2,10},{3,11},{4,12},{5,13},{6,14},{7,15},{8,0},{9,1},... | collective-permute-start | bytes 7077896 | tf_op jit(solution)/shard_map/ppermute | solution.py:11
  305.6 2.6 copy-start.3
Sparse Core Ops, SparseCore 0:
  10.7 56.3 all-gather.1
